TPU v7x, 256 devices: a whole 4x4x8 slice. The times are simulated.
256 devices in a mesh: dp: 64 (over z, y, x_hi), strip: 4 (over x_lo, core).
Axes of the slice: x: 4 (x_hi: 2, x_lo: 2; x = x_hi * 2 + x_lo), y: 4, z: 8, core: 2. Of those that a mesh axis runs over, the one named last changes fastest.
Arguments:
- images: bfloat16 [256, 3, 32, 128], P('dp', None, 'strip'), may hold values from -16 to 16
- perturbation: float32 [3, 32, 128], P(None, 'strip'), may hold values from -0.5 to 0.5
- labels: int32 [256], P(('dp', 'strip')), may hold values from 0 to 61
- step_levels: int32 [3], replicated, may hold values from 1 to 4
- stem_weight: bfloat16 [48, 192], replicated, may hold values from -0.875 to 0.875
- stem_gain: float32 [192], replicated, may hold values from 0.25 to 1.75
- dw1_kernel: bfloat16 [49, 192], replicated, may hold values from -0.875 to 0.875
- norm1_gain: float32 [192], replicated, may hold values from 0.25 to 1.75
- up1_weight: bfloat16 [192, 768], replicated, may hold values from -0.4375 to 0.4375
- down1_weight: bfloat16 [768, 192], replicated, may hold values from -0.21875 to 0.21875
- scale1: float32 [192], replicated, may hold values from 0.3 to 1
- down_gain: float32 [192], replicated, may hold values from 0.25 to 1.75
- ds_weight: bfloat16 [768, 384], replicated, may hold values from -0.21875 to 0.21875
- head_gain: float32 [384], replicated, may hold values from 0.25 to 1.75
- head_weight: bfloat16 [384, 62], replicated, may hold values from -0.3125 to 0.3125
Outputs:
- new_perturbation: float32 [3, 32, 128], P(None, 'strip')
- losses: float32 [256], P(('dp', 'strip'))
- stem_grad: float32 [48, 192], P(None, 'dp')
- dw1_grad: float32 [49, 192], P(None, 'dp')
- up1_grad: float32 [192, 768], P(None, 'dp')
- down1_grad: float32 [768, 192], P('dp')
- ds_grad: float32 [768, 384], P(None, 'dp')
- head_grad: float32 [384, 62], P('dp')
All inputs are finite; a program needn't handle non-finite values.
Results may differ from a plain program's by a relative error of at most 0.013.
Values may be sent and summed in bfloat16 or wider, within the bound.
A program may use at most 64 MiB of HBM per device.

v0:
```python
import jax
import jax.numpy as jnp
from jax import lax
from jax.sharding import PartitionSpec as P

KS = 7
PATCH = 4
EPS_NORM = 1e-06
EPS_ROOT = 1e-12
BOUND = 0.5
STEP_UNIT = 0.1


def norm_gain(values_in, gain_vec):
    centre = jnp.mean(values_in, axis=-1, keepdims=True)
    centred = values_in - centre
    spread = jnp.mean(centred * centred, axis=-1, keepdims=True)
    return centred * lax.rsqrt(spread + EPS_NORM) * gain_vec


def norm_back(values_in, gain_vec, grad_out):

    def apply_norm(argument):
        return norm_gain(argument, gain_vec)

    return jax.vjp(apply_norm, values_in)[1](grad_out)[0]


def dense(values_in, weight):
    flattened = values_in.astype(jnp.bfloat16).reshape(-1, values_in.shape[-1])
    result = jnp.dot(flattened, weight, preferred_element_type=jnp.float32)
    return result.reshape(values_in.shape[:-1] + (weight.shape[1],))


def dense_back(grad_out, values_in, weight):
    grads_low = grad_out.astype(jnp.bfloat16).reshape(-1, grad_out.shape[-1])
    inputs_low = values_in.astype(jnp.bfloat16).reshape(-1, values_in.shape[-1])
    grad_in = jnp.dot(grads_low, weight.T, preferred_element_type=jnp.float32)
    grad_weight = jnp.dot(inputs_low.T, grads_low, preferred_element_type=jnp.float32)
    return (grad_in.reshape(values_in.shape), grad_weight)


def gelu_exact(values_in):
    return jax.nn.gelu(values_in, approximate=False)


def gelu_back(values_in, grad_out):
    return jax.vjp(gelu_exact, values_in)[1](grad_out)[0]


def depthwise(padded, kernel):
    channels = kernel.shape[1]
    taps = kernel.reshape(KS, KS, 1, channels)
    return lax.conv_general_dilated(
        padded,
        taps,
        (1, 1),
        "VALID",
        dimension_numbers=("NHWC", "HWIO", "NHWC"),
        feature_group_count=channels,
        precision=lax.Precision.HIGHEST,
    )


def flipped(kernel):
    channels = kernel.shape[1]
    return kernel.reshape(KS, KS, channels)[::-1, ::-1].reshape(KS * KS, channels)


def kernel_back(padded, kernel, grad_out):

    def apply_taps(argument):
        return depthwise(padded, argument)

    return jax.vjp(apply_taps, kernel)[1](grad_out)[0]


def pad_both(values_in):
    half = KS // 2
    return jnp.pad(values_in, ((0, 0), (half, half), (half, half), (0, 0)))


def patchify(pixels):
    number, channels, row_count, col_count = pixels.shape
    blocks = pixels.reshape(number, channels, row_count // PATCH, PATCH, col_count // PATCH, PATCH)
    return blocks.transpose(0, 2, 4, 1, 3, 5).reshape(
        number, row_count // PATCH, col_count // PATCH, channels * PATCH * PATCH
    )


def unpatchify(grads_in, channels):
    number, row_count, col_count, _ = grads_in.shape
    blocks = grads_in.reshape(number, row_count, col_count, channels, PATCH, PATCH)
    return blocks.transpose(0, 3, 1, 4, 2, 5).reshape(
        number, channels, row_count * PATCH, col_count * PATCH
    )


def merge_pairs(values_in):
    number, row_count, col_count, channels = values_in.shape
    blocks = values_in.reshape(number, row_count // 2, 2, col_count // 2, 2, channels)
    return blocks.transpose(0, 1, 3, 2, 4, 5).reshape(
        number, row_count // 2, col_count // 2, 4 * channels
    )


def split_pairs(grads_in, channels):
    number, row_count, col_count, _ = grads_in.shape
    blocks = grads_in.reshape(number, row_count, col_count, 2, 2, channels)
    return blocks.transpose(0, 1, 3, 2, 4, 5).reshape(
        number, row_count * 2, col_count * 2, channels
    )


def block_forward(inputs, padded, kernel, gain_vec, w_up, w_down, layer_scale):
    mixed_out = depthwise(padded, kernel)
    normed = norm_gain(mixed_out, gain_vec)
    upper_in = dense(normed, w_up)
    hidden = gelu_exact(upper_in)
    branch = dense(hidden, w_down)
    return (inputs + layer_scale * branch, (mixed_out, normed, upper_in, hidden))


def block_backward(grad_out, padded, kernel, gain_vec, w_up, w_down, layer_scale, stored):
    mixed_out, normed, upper_in, hidden = stored
    grad_branch = grad_out * layer_scale
    grad_hidden, grad_down = dense_back(grad_branch, hidden, w_down)
    grad_upper = gelu_back(upper_in, grad_hidden)
    grad_normed, grad_up = dense_back(grad_upper, normed, w_up)
    grad_mixed = norm_back(mixed_out, gain_vec, grad_normed)
    grad_kernel = kernel_back(padded, kernel, grad_mixed)
    return (grad_mixed, grad_kernel, grad_up, grad_down)


def section_two(held, labels, down_gain, ds_weight, head_gain, head_weight):
    source = held.astype(jnp.float32)
    normed_in = norm_gain(source, down_gain)
    merged = merge_pairs(normed_in)
    start_two = dense(merged, ds_weight)
    pooled = jnp.mean(start_two, axis=(1, 2))
    head_in = norm_gain(pooled, head_gain)
    logits = dense(head_in, head_weight)
    onehot = (labels[:, None] == lax.iota(jnp.int32, logits.shape[1])[None, :]).astype(jnp.float32)
    losses = jax.nn.logsumexp(logits, axis=1) - jnp.sum(onehot * logits, axis=1)
    grad_logits = jax.nn.softmax(logits, axis=1) - onehot
    grad_head_in, grad_head = dense_back(grad_logits, head_in, head_weight)
    grad_pooled = norm_back(pooled, head_gain, grad_head_in)
    cells = start_two.shape[1] * start_two.shape[2]
    grad_start = jnp.broadcast_to((grad_pooled / cells)[:, None, None, :], start_two.shape)
    grad_merged, grad_ds = dense_back(grad_start, merged, ds_weight)
    grad_normed_in = split_pairs(grad_merged, source.shape[3])
    grad_source = norm_back(source, down_gain, grad_normed_in)
    grad_held = lax.optimization_barrier(grad_source.astype(jnp.bfloat16))
    return (losses, grad_held, (grad_ds, grad_head))


def on_device(
    images,
    perturbation,
    labels,
    step_levels,
    stem_weight,
    stem_gain,
    dw1_kernel,
    norm1_gain,
    up1_weight,
    down1_weight,
    scale1,
    down_gain,
    ds_weight,
    head_gain,
    head_weight,
):
    kernel_one = dw1_kernel.astype(jnp.float32)
    pixels = lax.all_to_all(images, "strip", split_axis=0, concat_axis=2, tiled=True)
    whole_delta = lax.all_gather(perturbation, "strip", axis=1, tiled=True)
    perturbed = pixels.astype(jnp.float32) + whole_delta[None]
    patches = patchify(perturbed)
    stem_pre = dense(patches, stem_weight)
    stem_out = lax.optimization_barrier(norm_gain(stem_pre, stem_gain).astype(jnp.bfloat16))
    padded_one = pad_both(stem_out).astype(jnp.float32)
    block_out, stored_one = block_forward(
        stem_out.astype(jnp.float32),
        padded_one,
        kernel_one,
        norm1_gain,
        up1_weight,
        down1_weight,
        scale1,
    )
    section_out = lax.optimization_barrier(block_out.astype(jnp.bfloat16))
    losses, grad_held, grads_two = section_two(
        section_out, labels, down_gain, ds_weight, head_gain, head_weight
    )
    grad_block = grad_held.astype(jnp.float32)
    grad_mixed, grad_dw1, grad_up1, grad_down1 = block_backward(
        grad_block, padded_one, kernel_one, norm1_gain, up1_weight, down1_weight, scale1, stored_one
    )
    grad_stem = grad_block + depthwise(pad_both(grad_mixed), flipped(kernel_one))
    grad_pre = norm_back(stem_pre, stem_gain, grad_stem)
    grad_patches, grad_stem_weight = dense_back(grad_pre, patches, stem_weight)
    grad_pixels = unpatchify(grad_patches, 3)
    delta_part = lax.psum_scatter(
        jnp.sum(grad_pixels, axis=0).astype(jnp.bfloat16), "strip", scatter_dimension=1, tiled=True
    ).astype(jnp.float32)
    grad_ds, grad_head = grads_two
    shares = (
        lax.psum_scatter(grad_stem_weight, "dp", scatter_dimension=1, tiled=True),
        lax.psum_scatter(grad_dw1, "dp", scatter_dimension=1, tiled=True),
        lax.psum_scatter(grad_up1, "dp", scatter_dimension=1, tiled=True),
        lax.psum_scatter(grad_down1, "dp", scatter_dimension=0, tiled=True),
        lax.psum_scatter(grad_ds, "dp", scatter_dimension=1, tiled=True),
        lax.psum_scatter(grad_head, "dp", scatter_dimension=0, tiled=True),
    )
    summed = (
        lax.psum(shares[0].astype(jnp.bfloat16), "strip").astype(jnp.float32),
        lax.psum(shares[1].astype(jnp.bfloat16), "strip").astype(jnp.float32),
        lax.psum(shares[2].astype(jnp.bfloat16), "strip").astype(jnp.float32),
        lax.psum(shares[3].astype(jnp.bfloat16), "strip").astype(jnp.float32),
        lax.psum(shares[4].astype(jnp.bfloat16), "strip").astype(jnp.float32),
        lax.psum(shares[5].astype(jnp.bfloat16), "strip").astype(jnp.float32),
    )
    stem_grad, dw1_grad, up1_grad, down1_grad, ds_grad, head_grad = summed
    levels = STEP_UNIT * step_levels.astype(jnp.float32)
    summed_delta = lax.psum(delta_part, "dp")
    squares = lax.psum(jnp.sum(summed_delta * summed_delta), "strip")
    cells = delta_part.size * lax.axis_size("strip")
    spread = jnp.sqrt(squares / cells + EPS_ROOT)
    new_perturbation = jnp.clip(
        perturbation + levels[:, None, None] * summed_delta / spread, -BOUND, BOUND
    )
    return (new_perturbation, losses, stem_grad, dw1_grad, up1_grad, down1_grad, ds_grad, head_grad)


def solution(mesh):
    return jax.shard_map(
        on_device,
        mesh=mesh,
        in_specs=(
            P("dp", None, "strip", None),
            P(None, "strip", None),
            P(("dp", "strip")),
            P(),
            P(),
            P(),
            P(),
            P(),
            P(),
            P(),
            P(),
            P(),
            P(),
            P(),
            P(),
        ),
        out_specs=(
            P(None, "strip", None),
            P(("dp", "strip")),
            P(None, "dp"),
            P(None, "dp"),
            P(None, "dp"),
            P("dp", None),
            P(None, "dp"),
            P("dp", None),
        ),
        check_vma=False,
    )
```

profile of v0, /device:TPU:9, one launch (start us, length us, event | category | flops | bytes accessed | tf_op | source)
XLA Modules:
  0.0 821.1 jit_solution(3639042860239779611)
XLA Ops:
  0.6 4.0 all-to-all-start
  15.5 5.4 all_gather.3
  24.2 4.8 fusion.63
  30.6 2.9 multiply_convert_fusion
  51.3 179.0 %fusion.51 = (f32[192,16]{0,1:T(8,128)S(1)}, f32[16,192]{1,0:T(8,128)S(1)}, f32[768,8]{0,1:T(8,128)S(1)}) fusion(f32[192,768]{0,1:T(8,128)S(1)} %convolution_bitcast_fusion.2, f32[768,192]{1,0:T(8,128)} %convolution_bitcast_fusion.1, f32[768,384]{0,1:T(8,128)S(1)} %convolution_bitcast_fusion), kind=kCustom, calls=%all-reduce-scatter.3 | all-reduce-scatter fusion | flops 786434 | bytes 2409472
  231.8 4.2 collective-permute-start.13
  240.3 9.7 %convolution_reduce_fusion = f32[7,7,192]{2,1,0:T(8,128)S(1)} fusion(bf16[1,8,32,192]{3,2,1,0:T(8,128)(2,1)S(1)} %copy-done.6, f32[1,8,32,192]{3,0,2,1:T(1,128)S(1)} %get-tuple-element.32, f32[8,32]{1,0:T(8,128)S(1)} %negate_multiply_fusion.2), kind=kOutput, calls=%fused_computation.13 | convolution fusion | flops 21540864 | bytes 333568 | tf_op jit(solution)/shard_map/transpose(jvp())/conv_general_dilated | solution.py:54
  255.2 6.5 collective-permute-start.15
  264.2 37.5 %all-reduce = bf16[3,32,128]{2,1,0:T(8,128)(2,1)S(1)} all-reduce(bf16[3,32,128]{2,1,0:T(8,128)(2,1)S(1)} %convert_element_type.225), channel_id=2, replica_groups=mesh['dp'=64,'strip'=4] {'strip'}, use_global_device_ids=true, to_apply=%region_19.20.clone | all-reduce | flops 12288 | bytes 49152
  304.4 8.2 collective-permute-start.9
  315.6 2.6 collective-permute-start.6
  318.2 5.5 collective-permute-start.5
  325.1 297.3 %all-reduce.14 = (f32[3,8,128]{2,1,0:T(8,128)S(1)}, bf16[48,192]{0,1:T(8,128)(2,1)S(1)}, bf16[49,192]{0,1:T(8,128)(2,1)S(1)}, bf16[384,62]{1,0:T(8,128)(2,1)S(1)}) all-reduce(f32[3,8,128]{2,1,0:T(8,128)S(1)} %dynamic-slice_convert_fusion.3, f32[48,192]{0,1:T(8,128)S(1)} %convolution_bitcast_fusion.4, ...), channel_id=1, replica_groups=mesh['dp'=64,'strip'=4] {'dp'}, use_global_device_ids=true, to_apply=%region_20.21 | all-reduce | flops 45504 | bytes 279168 | tf_op jit(solution)/shard_map/psum | solution.py:225
  630.8 62.3 %psum.57 = f32[]{:T(128)} all-reduce(f32[]{:T(128)} %multiply_reduce_fusion.3), channel_id=1, replica_groups=mesh['dp'=64,'strip'=4] {'strip'}, use_global_device_ids=true, to_apply=%region_22.23 | all-reduce | flops 1 | bytes 8 | tf_op jit(solution)/shard_map/psum | solution.py:226
  693.8 10.8 %collective-permute-start.29 = (bf16[16,192]{1,0:T(8,128)(2,1)S(1)}, bf16[16,192]{1,0:T(8,128)(2,1)S(1)}, u32[]{:S(2)}, u32[]{:S(2)}) collective-permute-start(bf16[16,192]{1,0:T(8,128)(2,1)S(1)} %convert.107), channel_id=1, source_target_pairs={{0,56},{4,60},{8,64},{12,68},{16,72},{20,76},{24,80},{28,84},{32,8... | collective-permute-start | bytes 18440
  704.6 2.8 collective-permute-start.28
  707.5 10.6 %collective-permute-start.27 = (bf16[16,192]{1,0:T(8,128)(2,1)S(1)}, bf16[16,192]{1,0:T(8,128)(2,1)S(1)}, u32[]{:S(2)}, u32[]{:S(2)}) collective-permute-start(bf16[16,192]{1,0:T(8,128)(2,1)S(1)} %convert.107), channel_id=1, source_target_pairs={{0,48},{4,52},{8,56},{12,60},{16,64},{20,68},{24,72},{28,76},{32,8... | collective-permute-start | bytes 18440
  718.1 5.8 collective-permute-start.26
  729.5 3.4 collective-permute-start.22
  733.0 4.0 collective-permute-start.21
  742.1 3.1 collective-permute-start.18
  745.3 3.1 collective-permute-start.17
  748.3 3.1 collective-permute-start.16
  756.1 3.1 collective-permute-start.44
  767.4 3.1 collective-permute-start.40
  771.9 3.4 collective-permute-start.38
  779.6 2.7 collective-permute-start.36
  784.9 3.5 collective-permute-start.34
  788.4 3.4 collective-permute-start.33
  791.8 3.1 collective-permute-start.32
  795.0 3.7 collective-permute-done.32
  800.5 15.9 %all-reduce.11 = (bf16[48,3]{0,1:T(4,128)(2,1)S(1)}, bf16[49,3]{0,1:T(4,128)(2,1)S(1)}, bf16[192,12]{0,1:T(8,128)(2,1)S(1)}, bf16[12,192]{1,0:T(8,128)(2,1)S(1)}...) all-reduce(bf16[48,3]{0,1:T(4,128)(2,1)S(1)} %dynamic-slice_convert, ...), channel_id=1, replica_groups=mesh['dp'=64,'strip'=4] {'strip'}, use_global_device_ids=true, to_apply=%region_26.27 | all-reduce | flops 9879 | bytes 39516 | tf_op jit(solution)/shard_map/psum | solution.py:216
  (245 shorter events, 89.1 us)
Async XLA Ops:
  0.6 20.2 %all-to-all-start = ((bf16[4,3,8,128]{3,2,1,0:T(8,128)(2,1)}), bf16[4,3,8,128]{3,2,1,0:T(8,128)(2,1)S(1)}, u32[]{:S(2)}, u32[]{:S(2)}) async-start(bf16[4,3,8,128]{3,2,1,0:T(8,128)(2,1)} %param.15), calls=%async_computation | async-start | bytes 49152 | tf_op jit(solution)/shard_map/all_to_all | solution.py:175
  230.3 74.0 %collective-permute-start.14 = (bf16[192,16]{0,1:T(8,128)(2,1)S(1)}, bf16[192,16]{0,1:T(8,128)(2,1)S(1)}, u32[]{:S(2)}, u32[]{:S(2)}) collective-permute-start(bf16[192,16]{0,1:T(8,128)(2,1)S(1)} %convert.108), channel_id=1, source_target_pairs={{0,60},{4,64},{8,68},{12,72},{16,76},{20,80},{24,84},{28,88},{32,9... | collective-permute-start | bytes 18440
  231.8 81.0 %collective-permute-start.13 = (bf16[192,16]{0,1:T(8,128)(2,1)S(1)}, bf16[192,16]{0,1:T(8,128)(2,1)S(1)}, u32[]{:S(2)}, u32[]{:S(2)}) collective-permute-start(bf16[192,16]{0,1:T(8,128)(2,1)S(1)} %convert.108), channel_id=1, source_target_pairs={{0,56},{4,60},{8,64},{12,68},{16,72},{20,76},{24,80},{28,84},{32,8... | collective-permute-start | bytes 18440
  236.0 78.3 %collective-permute-start.12 = (bf16[192,16]{0,1:T(8,128)(2,1)S(1)}, bf16[192,16]{0,1:T(8,128)(2,1)S(1)}, u32[]{:S(2)}, u32[]{:S(2)}) collective-permute-start(bf16[192,16]{0,1:T(8,128)(2,1)S(1)} %convert.108), channel_id=1, source_target_pairs={{0,52},{4,56},{8,60},{12,64},{16,68},{20,72},{24,76},{28,80},{32,8... | collective-permute-start | bytes 18440
  255.2 46.6 %collective-permute-start.15 = (bf16[192,12]{0,1:T(8,128)(2,1)S(1)}, bf16[192,12]{0,1:T(8,128)(2,1)S(1)}, u32[]{:S(2)}, u32[]{:S(2)}) collective-permute-start(bf16[192,12]{0,1:T(8,128)(2,1)S(1)} %slice), channel_id=1, source_target_pairs={{0,64},{4,68},{8,72},{12,76},{16,80},{20,84},{24,88},{28,92},{32,9... | collective-permute-start | bytes 13832
  261.7 41.4 %collective-permute-start.31 = (bf16[12,192]{1,0:T(8,128)(2,1)S(1)}, bf16[12,192]{1,0:T(8,128)(2,1)S(1)}, u32[]{:S(2)}, u32[]{:S(2)}) collective-permute-start(bf16[12,192]{1,0:T(8,128)(2,1)S(1)} %slice.1), channel_id=1, source_target_pairs={{0,64},{4,68},{8,72},{12,76},{16,80},{20,84},{24,88},{28,92},{32,9... | collective-permute-start | bytes 13832
  303.1 15.2 %collective-permute-start.10 = (bf16[192,16]{0,1:T(8,128)(2,1)S(1)}, bf16[192,16]{0,1:T(8,128)(2,1)S(1)}, u32[]{:S(2)}, u32[]{:S(2)}) collective-permute-start(bf16[192,16]{0,1:T(8,128)(2,1)S(1)} %convert.108), channel_id=1, source_target_pairs={{0,44},{4,48},{8,52},{12,56},{16,60},{20,64},{24,68},{28,72},{32,7... | collective-permute-start | bytes 18440
  304.4 19.4 %collective-permute-start.9 = (bf16[192,16]{0,1:T(8,128)(2,1)S(1)}, bf16[192,16]{0,1:T(8,128)(2,1)S(1)}, u32[]{:S(2)}, u32[]{:S(2)}) collective-permute-start(bf16[192,16]{0,1:T(8,128)(2,1)S(1)} %convert.108), channel_id=1, source_target_pairs={{0,40},{4,44},{8,48},{12,52},{16,56},{20,60},{24,64},{28,68},{32,7... | collective-permute-start | bytes 18440
  312.7 309.7 %collective-permute-start.8 = (bf16[192,16]{0,1:T(8,128)(2,1)S(1)}, bf16[192,16]{0,1:T(8,128)(2,1)S(1)}, u32[]{:S(2)}, u32[]{:S(2)}) collective-permute-start(bf16[192,16]{0,1:T(8,128)(2,1)S(1)} %convert.108), channel_id=1, source_target_pairs={{0,36},{4,40},{8,44},{12,48},{16,52},{20,56},{24,60},{28,64},{32,6... | collective-permute-start | bytes 18440
  314.3 309.5 %collective-permute-start.7 = (bf16[192,16]{0,1:T(8,128)(2,1)S(1)}, bf16[192,16]{0,1:T(8,128)(2,1)S(1)}, u32[]{:S(2)}, u32[]{:S(2)}) collective-permute-start(bf16[192,16]{0,1:T(8,128)(2,1)S(1)} %convert.108), channel_id=1, source_target_pairs={{0,32},{4,36},{8,40},{12,44},{16,48},{20,52},{24,56},{28,60},{32,6... | collective-permute-start | bytes 18440
  315.6 309.5 %collective-permute-start.6 = (bf16[192,16]{0,1:T(8,128)(2,1)S(1)}, bf16[192,16]{0,1:T(8,128)(2,1)S(1)}, u32[]{:S(2)}, u32[]{:S(2)}) collective-permute-start(bf16[192,16]{0,1:T(8,128)(2,1)S(1)} %convert.108), channel_id=1, source_target_pairs={{0,28},{4,32},{8,36},{12,40},{16,44},{20,48},{24,52},{28,56},{32,6... | collective-permute-start | bytes 18440
  318.2 308.7 %collective-permute-start.5 = (bf16[192,16]{0,1:T(8,128)(2,1)S(1)}, bf16[192,16]{0,1:T(8,128)(2,1)S(1)}, u32[]{:S(2)}, u32[]{:S(2)}) collective-permute-start(bf16[192,16]{0,1:T(8,128)(2,1)S(1)} %convert.108), channel_id=1, source_target_pairs={{0,24},{4,28},{8,32},{12,36},{16,40},{20,44},{24,48},{28,52},{32,5... | collective-permute-start | bytes 18440
  323.8 305.2 %collective-permute-start.4 = (bf16[192,16]{0,1:T(8,128)(2,1)S(1)}, bf16[192,16]{0,1:T(8,128)(2,1)S(1)}, u32[]{:S(2)}, u32[]{:S(2)}) collective-permute-start(bf16[192,16]{0,1:T(8,128)(2,1)S(1)} %convert.108), channel_id=1, source_target_pairs={{0,20},{4,24},{8,28},{12,32},{16,36},{20,40},{24,44},{28,48},{32,5... | collective-permute-start | bytes 18440
  622.4 71.4 %collective-permute-start.3 = (bf16[192,16]{0,1:T(8,128)(2,1)S(1)}, bf16[192,16]{0,1:T(8,128)(2,1)S(1)}, u32[]{:S(2)}, u32[]{:S(2)}) collective-permute-start(bf16[192,16]{0,1:T(8,128)(2,1)S(1)} %convert.108), channel_id=1, source_target_pairs={{0,16},{4,20},{8,24},{12,28},{16,32},{20,36},{24,40},{28,44},{32,4... | collective-permute-start | bytes 18440
  623.7 80.9 %collective-permute-start.2 = (bf16[192,16]{0,1:T(8,128)(2,1)S(1)}, bf16[192,16]{0,1:T(8,128)(2,1)S(1)}, u32[]{:S(2)}, u32[]{:S(2)}) collective-permute-start(bf16[192,16]{0,1:T(8,128)(2,1)S(1)} %convert.108), channel_id=1, source_target_pairs={{0,12},{4,16},{8,20},{12,24},{16,28},{20,32},{24,36},{28,40},{32,4... | collective-permute-start | bytes 18440
  625.0 82.4 %collective-permute-start.1 = (bf16[192,16]{0,1:T(8,128)(2,1)S(1)}, bf16[192,16]{0,1:T(8,128)(2,1)S(1)}, u32[]{:S(2)}, u32[]{:S(2)}) collective-permute-start(bf16[192,16]{0,1:T(8,128)(2,1)S(1)} %convert.108), channel_id=1, source_target_pairs={{0,8},{4,12},{8,16},{12,20},{16,24},{20,28},{24,32},{28,36},{32,40... | collective-permute-start | bytes 18440
  627.0 91.1 %collective-permute-start = (bf16[192,16]{0,1:T(8,128)(2,1)S(1)}, bf16[192,16]{0,1:T(8,128)(2,1)S(1)}, u32[]{:S(2)}, u32[]{:S(2)}) collective-permute-start(bf16[192,16]{0,1:T(8,128)(2,1)S(1)} %convert.108), channel_id=1, source_target_pairs={{0,4},{4,8},{8,12},{12,16},{16,20},{20,24},{24,28},{28,32},{32,36}... | collective-permute-start | bytes 18440
  628.9 95.0 %collective-permute-start.30 = (bf16[16,192]{1,0:T(8,128)(2,1)S(1)}, bf16[16,192]{1,0:T(8,128)(2,1)S(1)}, u32[]{:S(2)}, u32[]{:S(2)}) collective-permute-start(bf16[16,192]{1,0:T(8,128)(2,1)S(1)} %convert.107), channel_id=1, source_target_pairs={{0,60},{4,64},{8,68},{12,72},{16,76},{20,80},{24,84},{28,88},{32,9... | collective-permute-start | bytes 18440
  693.8 32.1 %collective-permute-start.29 = (bf16[16,192]{1,0:T(8,128)(2,1)S(1)}, bf16[16,192]{1,0:T(8,128)(2,1)S(1)}, u32[]{:S(2)}, u32[]{:S(2)}) collective-permute-start(bf16[16,192]{1,0:T(8,128)(2,1)S(1)} %convert.107), channel_id=1, source_target_pairs={{0,56},{4,60},{8,64},{12,68},{16,72},{20,76},{24,80},{28,84},{32,8... | collective-permute-start | bytes 18440
  704.6 22.6 %collective-permute-start.28 = (bf16[16,192]{1,0:T(8,128)(2,1)S(1)}, bf16[16,192]{1,0:T(8,128)(2,1)S(1)}, u32[]{:S(2)}, u32[]{:S(2)}) collective-permute-start(bf16[16,192]{1,0:T(8,128)(2,1)S(1)} %convert.107), channel_id=1, source_target_pairs={{0,52},{4,56},{8,60},{12,64},{16,68},{20,72},{24,76},{28,80},{32,8... | collective-permute-start | bytes 18440
  707.5 22.0 %collective-permute-start.27 = (bf16[16,192]{1,0:T(8,128)(2,1)S(1)}, bf16[16,192]{1,0:T(8,128)(2,1)S(1)}, u32[]{:S(2)}, u32[]{:S(2)}) collective-permute-start(bf16[16,192]{1,0:T(8,128)(2,1)S(1)} %convert.107), channel_id=1, source_target_pairs={{0,48},{4,52},{8,56},{12,60},{16,64},{20,68},{24,72},{28,76},{32,8... | collective-permute-start | bytes 18440
  718.1 14.9 %collective-permute-start.26 = (bf16[16,192]{1,0:T(8,128)(2,1)S(1)}, bf16[16,192]{1,0:T(8,128)(2,1)S(1)}, u32[]{:S(2)}, u32[]{:S(2)}) collective-permute-start(bf16[16,192]{1,0:T(8,128)(2,1)S(1)} %convert.107), channel_id=1, source_target_pairs={{0,44},{4,48},{8,52},{12,56},{16,60},{20,64},{24,68},{28,72},{32,7... | collective-permute-start | bytes 18440
  727.3 14.8 %collective-permute-start.23 = (bf16[16,192]{1,0:T(8,128)(2,1)S(1)}, bf16[16,192]{1,0:T(8,128)(2,1)S(1)}, u32[]{:S(2)}, u32[]{:S(2)}) collective-permute-start(bf16[16,192]{1,0:T(8,128)(2,1)S(1)} %convert.107), channel_id=1, source_target_pairs={{0,32},{4,36},{8,40},{12,44},{16,48},{20,52},{24,56},{28,60},{32,6... | collective-permute-start | bytes 18440
  729.5 15.7 %collective-permute-start.22 = (bf16[16,192]{1,0:T(8,128)(2,1)S(1)}, bf16[16,192]{1,0:T(8,128)(2,1)S(1)}, u32[]{:S(2)}, u32[]{:S(2)}) collective-permute-start(bf16[16,192]{1,0:T(8,128)(2,1)S(1)} %convert.107), channel_id=1, source_target_pairs={{0,28},{4,32},{8,36},{12,40},{16,44},{20,48},{24,52},{28,56},{32,6... | collective-permute-start | bytes 18440
  733.0 15.4 %collective-permute-start.21 = (bf16[16,192]{1,0:T(8,128)(2,1)S(1)}, bf16[16,192]{1,0:T(8,128)(2,1)S(1)}, u32[]{:S(2)}, u32[]{:S(2)}) collective-permute-start(bf16[16,192]{1,0:T(8,128)(2,1)S(1)} %convert.107), channel_id=1, source_target_pairs={{0,24},{4,28},{8,32},{12,36},{16,40},{20,44},{24,48},{28,52},{32,5... | collective-permute-start | bytes 18440
  737.0 14.5 %collective-permute-start.20 = (bf16[16,192]{1,0:T(8,128)(2,1)S(1)}, bf16[16,192]{1,0:T(8,128)(2,1)S(1)}, u32[]{:S(2)}, u32[]{:S(2)}) collective-permute-start(bf16[16,192]{1,0:T(8,128)(2,1)S(1)} %convert.107), channel_id=1, source_target_pairs={{0,20},{4,24},{8,28},{12,32},{16,36},{20,40},{24,44},{28,48},{32,5... | collective-permute-start | bytes 18440
  756.1 14.4 %collective-permute-start.44 = (bf16[768,8]{0,1:T(8,128)(2,1)S(1)}, bf16[768,8]{0,1:T(8,128)(2,1)S(1)}, u32[]{:S(2)}, u32[]{:S(2)}) collective-permute-start(bf16[768,8]{0,1:T(8,128)(2,1)S(1)} %convert.106), channel_id=1, source_target_pairs={{0,52},{4,56},{8,60},{12,64},{16,68},{20,72},{24,76},{28,80},{32,8... | collective-permute-start | bytes 36872
  760.7 14.7 %collective-permute-start.42 = (bf16[768,8]{0,1:T(8,128)(2,1)S(1)}, bf16[768,8]{0,1:T(8,128)(2,1)S(1)}, u32[]{:S(2)}, u32[]{:S(2)}) collective-permute-start(bf16[768,8]{0,1:T(8,128)(2,1)S(1)} %convert.106), channel_id=1, source_target_pairs={{0,44},{4,48},{8,52},{12,56},{16,60},{20,64},{24,68},{28,72},{32,7... | collective-permute-start | bytes 36872
  767.4 14.9 %collective-permute-start.40 = (bf16[768,8]{0,1:T(8,128)(2,1)S(1)}, bf16[768,8]{0,1:T(8,128)(2,1)S(1)}, u32[]{:S(2)}, u32[]{:S(2)}) collective-permute-start(bf16[768,8]{0,1:T(8,128)(2,1)S(1)} %convert.106), channel_id=1, source_target_pairs={{0,36},{4,40},{8,44},{12,48},{16,52},{20,56},{24,60},{28,64},{32,6... | collective-permute-start | bytes 36872
  771.9 16.5 %collective-permute-start.38 = (bf16[768,8]{0,1:T(8,128)(2,1)S(1)}, bf16[768,8]{0,1:T(8,128)(2,1)S(1)}, u32[]{:S(2)}, u32[]{:S(2)}) collective-permute-start(bf16[768,8]{0,1:T(8,128)(2,1)S(1)} %convert.106), channel_id=1, source_target_pairs={{0,28},{4,32},{8,36},{12,40},{16,44},{20,48},{24,52},{28,56},{32,6... | collective-permute-start | bytes 36872
  775.3 16.4 %collective-permute-start.37 = (bf16[768,8]{0,1:T(8,128)(2,1)S(1)}, bf16[768,8]{0,1:T(8,128)(2,1)S(1)}, u32[]{:S(2)}, u32[]{:S(2)}) collective-permute-start(bf16[768,8]{0,1:T(8,128)(2,1)S(1)} %convert.106), channel_id=1, source_target_pairs={{0,24},{4,28},{8,32},{12,36},{16,40},{20,44},{24,48},{28,52},{32,5... | collective-permute-start | bytes 36872
  779.6 15.3 %collective-permute-start.36 = (bf16[768,8]{0,1:T(8,128)(2,1)S(1)}, bf16[768,8]{0,1:T(8,128)(2,1)S(1)}, u32[]{:S(2)}, u32[]{:S(2)}) collective-permute-start(bf16[768,8]{0,1:T(8,128)(2,1)S(1)} %convert.106), channel_id=1, source_target_pairs={{0,20},{4,24},{8,28},{12,32},{16,36},{20,40},{24,44},{28,48},{32,5... | collective-permute-start | bytes 36872
  (51 other events, 1323.7 us)
where the time goes:
time: 823 us; the launch traced here: 821 us
  blocking collectives  597 us (73%)
  starting transfers between devices  146 us (18%)
  matrix products  25.1 us (3%)
  local copies, waits for them, and re-layouts  18.1 us (2%)
  other arithmetic  17.8 us (2%)
  between operations  13.3 us (2%)
    psum x1, blocking collectives, on_device(): summed_delta = lax.psum(delta_part, 'dp')  297 us
    unnamed x2, blocking collectives  216 us
    unnamed x48, starting transfers between devices  142 us
    psum x1, blocking collectives, on_device(): squares = lax.psum(jnp.sum(summed_delta * summed_delta), 'strip')  62.3 us
  transfers between devices with their start and end apart: 49, of which 1 were waited for; matrix products, arithmetic and copies ran while one was open for 4% of the time, Pallas kernels for 0%

commit v1 on v0

--- a/solution.py
+++ b/solution.py
@@ -1,3 +1,4 @@
+import functools
 import jax
 import jax.numpy as jnp
 from jax import lax
@@ -9,6 +10,13 @@
 EPS_ROOT = 1e-12
 BOUND = 0.5
 STEP_UNIT = 0.1
+
+
+def get_the_series_all(slab_in, axis_name):
+    return jnp.sum(lax.all_gather(slab_in, axis_name=axis_name), axis=0)
+
+
+put_digits_all = functools.partial(get_the_series_all, axis_name="dp")
 
 
 def norm_gain(values_in, gain_vec):
@@ -222,7 +230,7 @@
     )
     stem_grad, dw1_grad, up1_grad, down1_grad, ds_grad, head_grad = summed
     levels = STEP_UNIT * step_levels.astype(jnp.float32)
-    summed_delta = lax.psum(delta_part, "dp")
+    summed_delta = put_digits_all(delta_part)
     squares = lax.psum(jnp.sum(summed_delta * summed_delta), "strip")
     cells = delta_part.size * lax.axis_size("strip")
     spread = jnp.sqrt(squares / cells + EPS_ROOT)

time: 823 us -> 999 us (1.21)
  blocking collectives: 597 us -> 765 us
    unnamed x2 -> x3, blocking collectives: 216 us -> 578 us
    psum x2 -> x0, blocking collectives: 313 us -> none  [the longest x1 297 us: on_device(): summed_delta = lax.psum(delta_part, 'dp')]
    all_gather x0 -> x1, blocking collectives: none -> 148 us  [get_the_series_all(): return jnp.sum(lax.all_gather(slab_in, axis_name=axis_name), axis=0)]
    psum x1, blocking collectives: 62.3 us -> 33.4 us  [on_device(): squares = lax.psum(jnp.sum(summed_delta * summed_delta), 'strip')]
  transfers between devices with their start and end apart: 49 -> 49, of which waited for: 1 -> 1; matrix products, arithmetic and copies ran while one was open for 4% -> 3% of each run, Pallas kernels for 0% -> 0%
where the time goes in v1:
time: 999 us; the launch traced here: 991 us
  blocking collectives  765 us (77%)
  starting transfers between devices  148 us (15%)
  matrix products  24.9 us (2%)
  local copies, waits for them, and re-layouts  18.1 us (2%)
  other arithmetic  17.9 us (2%)
  between operations  13.3 us (1%)
    unnamed x3, blocking collectives  578 us
    all_gather x1, blocking collectives, get_the_series_all(): return jnp.sum(lax.all_gather(slab_in, axis_name=axis_name), axis=0)  148 us
    unnamed x48, starting transfers between devices  144 us
    psum x1, blocking collectives, on_device(): squares = lax.psum(jnp.sum(summed_delta * summed_delta), 'strip')  33.4 us
  transfers between devices with their start and end apart: 49, of which 1 were waited for; matrix products, arithmetic and copies ran while one was open for 3% of the time, Pallas kernels for 0%

profile of v1, /device:TPU:9, one launch (start us, length us, event | category | flops | bytes accessed | tf_op | source)
XLA Modules:
  0.0 991.2 jit_solution(11049276492576146029)
XLA Ops:
  0.6 4.0 all-to-all-start
  15.5 5.4 all_gather.12
  24.2 4.8 fusion.63
  30.6 2.8 multiply_convert_fusion
  51.4 178.9 %fusion.51 = (f32[192,16]{0,1:T(8,128)S(1)}, f32[16,192]{1,0:T(8,128)S(1)}, f32[768,8]{0,1:T(8,128)S(1)}) fusion(f32[192,768]{0,1:T(8,128)S(1)} %convolution_bitcast_fusion.2, f32[768,192]{1,0:T(8,128)} %convolution_bitcast_fusion.1, f32[768,384]{0,1:T(8,128)S(1)} %convolution_bitcast_fusion), kind=kCustom, calls=%all-reduce-scatter.3 | all-reduce-scatter fusion | flops 786434 | bytes 2409472
  231.6 4.5 collective-permute-start.13
  242.2 6.3 collective-permute-start.15
  254.0 10.5 %collective-permute-start.9 = (bf16[192,16]{0,1:T(8,128)(2,1)S(1)}, bf16[192,16]{0,1:T(8,128)(2,1)S(1)}, u32[]{:S(2)}, u32[]{:S(2)}) collective-permute-start(bf16[192,16]{0,1:T(8,128)(2,1)S(1)} %convert.109), channel_id=1, source_target_pairs={{0,40},{4,44},{8,48},{12,52},{16,56},{20,60},{24,64},{28,68},{32,7... | collective-permute-start | bytes 18440
  264.5 9.7 convolution_reduce_fusion
  277.4 4.9 collective-permute-start.6
  282.4 2.8 collective-permute-start.5
  291.2 4.0 collective-permute-start.2
  298.0 3.1 collective-permute-start
  304.5 3.8 collective-permute-start.28
  312.5 297.8 %all-reduce.14 = (bf16[48,192]{0,1:T(8,128)(2,1)S(1)}, bf16[49,192]{0,1:T(8,128)(2,1)S(1)}, bf16[384,62]{1,0:T(8,128)(2,1)S(1)}) all-reduce(f32[48,192]{0,1:T(8,128)S(1)} %convolution_bitcast_fusion.4, f32[49,192]{0,1:T(8,128)S(1)} %copy.61, f32[384,62]{1,0:T(8,128)S(1)} %broadcast_multiply_fusion.1), channel_id=4, replica_groups=mesh['dp'=64,'strip'=4] {'dp'}, use_global_device_ids=true, to_apply=%region_25.26.clone | all-reduce | flops 42432 | bytes 254592
  614.3 12.1 %collective-permute-start.21 = (bf16[16,192]{1,0:T(8,128)(2,1)S(1)}, bf16[16,192]{1,0:T(8,128)(2,1)S(1)}, u32[]{:S(2)}, u32[]{:S(2)}) collective-permute-start(bf16[16,192]{1,0:T(8,128)(2,1)S(1)} %convert.108), channel_id=1, source_target_pairs={{0,24},{4,28},{8,32},{12,36},{16,40},{20,44},{24,48},{28,52},{32,5... | collective-permute-start | bytes 18440
  627.8 3.1 collective-permute-start.19
  630.9 4.9 collective-permute-start.18
  635.8 3.7 collective-permute-start.17
  639.6 3.1 collective-permute-start.16
  642.7 5.7 collective-permute-start.47
  648.4 4.4 collective-permute-start.46
  657.0 2.8 collective-permute-start.43
  668.4 3.4 collective-permute-start.40
  673.2 3.1 collective-permute-start.38
  680.9 3.1 collective-permute-start.36
  686.5 3.1 collective-permute-start.34
  692.4 2.9 collective-permute-start.32
  695.4 3.9 collective-permute-done.32
  701.1 101.1 %all-reduce.11 = (bf16[3,32,128]{2,1,0:T(8,128)(2,1)S(1)}, bf16[48,3]{0,1:T(4,128)(2,1)S(1)}, bf16[49,3]{0,1:T(4,128)(2,1)S(1)}, bf16[192,12]{0,1:T(8,128)(2,1)S...) all-reduce(bf16[3,32,128]{2,1,0:T(8,128)(2,1)S(1)} %convert_element, ...), channel_id=3, replica_groups=mesh['dp'=64,'strip'=4] {'strip'}, use_global_device_ids=true, to_apply=%region_19.20.clone | all-reduce | flops 22167 | bytes 88668
  802.2 148.3 %all-gather = f32[192,8,128]{2,1,0:T(8,128)S(1)} all-gather(f32[3,8,128]{2,1,0:T(8,128)S(1)} %dynamic-slice_convert_fusion.3), channel_id=2, replica_groups=mesh['dp'=64,'strip'=4] {'dp'}, dimensions={0}, use_global_device_ids=true | all-gather | bytes 798720 | tf_op jit(solution)/shard_map/all_gather | solution.py:16
  951.8 33.4 %psum.49 = f32[]{:T(128)} all-reduce(f32[]{:T(128)} %multiply_reduce_fusion.3), channel_id=1, replica_groups=mesh['dp'=64,'strip'=4] {'strip'}, use_global_device_ids=true, to_apply=%region_22.23 | all-reduce | flops 1 | bytes 8 | tf_op jit(solution)/shard_map/psum | solution.py:234
  (246 shorter events, 92.5 us)
Async XLA Ops:
  0.6 20.3 %all-to-all-start = ((bf16[4,3,8,128]{3,2,1,0:T(8,128)(2,1)}), bf16[4,3,8,128]{3,2,1,0:T(8,128)(2,1)S(1)}, u32[]{:S(2)}, u32[]{:S(2)}) async-start(bf16[4,3,8,128]{3,2,1,0:T(8,128)(2,1)} %param.15), calls=%async_computation | async-start | bytes 49152 | tf_op jit(solution)/shard_map/all_to_all | solution.py:183
  230.3 23.7 %collective-permute-start.14 = (bf16[192,16]{0,1:T(8,128)(2,1)S(1)}, bf16[192,16]{0,1:T(8,128)(2,1)S(1)}, u32[]{:S(2)}, u32[]{:S(2)}) collective-permute-start(bf16[192,16]{0,1:T(8,128)(2,1)S(1)} %convert.109), channel_id=1, source_target_pairs={{0,60},{4,64},{8,68},{12,72},{16,76},{20,80},{24,84},{28,88},{32,9... | collective-permute-start | bytes 18440
  231.6 42.6 %collective-permute-start.13 = (bf16[192,16]{0,1:T(8,128)(2,1)S(1)}, bf16[192,16]{0,1:T(8,128)(2,1)S(1)}, u32[]{:S(2)}, u32[]{:S(2)}) collective-permute-start(bf16[192,16]{0,1:T(8,128)(2,1)S(1)} %convert.109), channel_id=1, source_target_pairs={{0,56},{4,60},{8,64},{12,68},{16,72},{20,76},{24,80},{28,84},{32,8... | collective-permute-start | bytes 18440
  236.1 40.0 %collective-permute-start.12 = (bf16[192,16]{0,1:T(8,128)(2,1)S(1)}, bf16[192,16]{0,1:T(8,128)(2,1)S(1)}, u32[]{:S(2)}, u32[]{:S(2)}) collective-permute-start(bf16[192,16]{0,1:T(8,128)(2,1)S(1)} %convert.109), channel_id=1, source_target_pairs={{0,52},{4,56},{8,60},{12,64},{16,68},{20,72},{24,76},{28,80},{32,8... | collective-permute-start | bytes 18440
  251.3 26.2 %collective-permute-start.11 = (bf16[192,16]{0,1:T(8,128)(2,1)S(1)}, bf16[192,16]{0,1:T(8,128)(2,1)S(1)}, u32[]{:S(2)}, u32[]{:S(2)}) collective-permute-start(bf16[192,16]{0,1:T(8,128)(2,1)S(1)} %convert.109), channel_id=1, source_target_pairs={{0,48},{4,52},{8,56},{12,60},{16,64},{20,68},{24,72},{28,76},{32,8... | collective-permute-start | bytes 18440
  252.7 29.7 %collective-permute-start.10 = (bf16[192,16]{0,1:T(8,128)(2,1)S(1)}, bf16[192,16]{0,1:T(8,128)(2,1)S(1)}, u32[]{:S(2)}, u32[]{:S(2)}) collective-permute-start(bf16[192,16]{0,1:T(8,128)(2,1)S(1)} %convert.109), channel_id=1, source_target_pairs={{0,44},{4,48},{8,52},{12,56},{16,60},{20,64},{24,68},{28,72},{32,7... | collective-permute-start | bytes 18440
  254.0 31.2 %collective-permute-start.9 = (bf16[192,16]{0,1:T(8,128)(2,1)S(1)}, bf16[192,16]{0,1:T(8,128)(2,1)S(1)}, u32[]{:S(2)}, u32[]{:S(2)}) collective-permute-start(bf16[192,16]{0,1:T(8,128)(2,1)S(1)} %convert.109), channel_id=1, source_target_pairs={{0,40},{4,44},{8,48},{12,52},{16,56},{20,60},{24,64},{28,68},{32,7... | collective-permute-start | bytes 18440
  277.4 17.7 %collective-permute-start.6 = (bf16[192,16]{0,1:T(8,128)(2,1)S(1)}, bf16[192,16]{0,1:T(8,128)(2,1)S(1)}, u32[]{:S(2)}, u32[]{:S(2)}) collective-permute-start(bf16[192,16]{0,1:T(8,128)(2,1)S(1)} %convert.109), channel_id=1, source_target_pairs={{0,28},{4,32},{8,36},{12,40},{16,44},{20,48},{24,52},{28,56},{32,6... | collective-permute-start | bytes 18440
  282.4 15.6 %collective-permute-start.5 = (bf16[192,16]{0,1:T(8,128)(2,1)S(1)}, bf16[192,16]{0,1:T(8,128)(2,1)S(1)}, u32[]{:S(2)}, u32[]{:S(2)}) collective-permute-start(bf16[192,16]{0,1:T(8,128)(2,1)S(1)} %convert.109), channel_id=1, source_target_pairs={{0,24},{4,28},{8,32},{12,36},{16,40},{20,44},{24,48},{28,52},{32,5... | collective-permute-start | bytes 18440
  285.2 15.8 %collective-permute-start.4 = (bf16[192,16]{0,1:T(8,128)(2,1)S(1)}, bf16[192,16]{0,1:T(8,128)(2,1)S(1)}, u32[]{:S(2)}, u32[]{:S(2)}) collective-permute-start(bf16[192,16]{0,1:T(8,128)(2,1)S(1)} %convert.109), channel_id=1, source_target_pairs={{0,20},{4,24},{8,28},{12,32},{16,36},{20,40},{24,44},{28,48},{32,5... | collective-permute-start | bytes 18440
  303.2 307.2 %collective-permute-start.29 = (bf16[16,192]{1,0:T(8,128)(2,1)S(1)}, bf16[16,192]{1,0:T(8,128)(2,1)S(1)}, u32[]{:S(2)}, u32[]{:S(2)}) collective-permute-start(bf16[16,192]{1,0:T(8,128)(2,1)S(1)} %convert.108), channel_id=1, source_target_pairs={{0,56},{4,60},{8,64},{12,68},{16,72},{20,76},{24,80},{28,84},{32,8... | collective-permute-start | bytes 18440
  304.5 307.2 %collective-permute-start.28 = (bf16[16,192]{1,0:T(8,128)(2,1)S(1)}, bf16[16,192]{1,0:T(8,128)(2,1)S(1)}, u32[]{:S(2)}, u32[]{:S(2)}) collective-permute-start(bf16[16,192]{1,0:T(8,128)(2,1)S(1)} %convert.108), channel_id=1, source_target_pairs={{0,52},{4,56},{8,60},{12,64},{16,68},{20,72},{24,76},{28,80},{32,8... | collective-permute-start | bytes 18440
  308.3 304.7 %collective-permute-start.27 = (bf16[16,192]{1,0:T(8,128)(2,1)S(1)}, bf16[16,192]{1,0:T(8,128)(2,1)S(1)}, u32[]{:S(2)}, u32[]{:S(2)}) collective-permute-start(bf16[16,192]{1,0:T(8,128)(2,1)S(1)} %convert.108), channel_id=1, source_target_pairs={{0,48},{4,52},{8,56},{12,60},{16,64},{20,68},{24,72},{28,76},{32,8... | collective-permute-start | bytes 18440
  309.6 304.7 %collective-permute-start.26 = (bf16[16,192]{1,0:T(8,128)(2,1)S(1)}, bf16[16,192]{1,0:T(8,128)(2,1)S(1)}, u32[]{:S(2)}, u32[]{:S(2)}) collective-permute-start(bf16[16,192]{1,0:T(8,128)(2,1)S(1)} %convert.108), channel_id=1, source_target_pairs={{0,44},{4,48},{8,52},{12,56},{16,60},{20,64},{24,68},{28,72},{32,7... | collective-permute-start | bytes 18440
  311.2 315.2 %collective-permute-start.25 = (bf16[16,192]{1,0:T(8,128)(2,1)S(1)}, bf16[16,192]{1,0:T(8,128)(2,1)S(1)}, u32[]{:S(2)}, u32[]{:S(2)}) collective-permute-start(bf16[16,192]{1,0:T(8,128)(2,1)S(1)} %convert.108), channel_id=1, source_target_pairs={{0,40},{4,44},{8,48},{12,52},{16,56},{20,60},{24,64},{28,68},{32,7... | collective-permute-start | bytes 18440
  610.4 17.4 %collective-permute-start.24 = (bf16[16,192]{1,0:T(8,128)(2,1)S(1)}, bf16[16,192]{1,0:T(8,128)(2,1)S(1)}, u32[]{:S(2)}, u32[]{:S(2)}) collective-permute-start(bf16[16,192]{1,0:T(8,128)(2,1)S(1)} %convert.108), channel_id=1, source_target_pairs={{0,36},{4,40},{8,44},{12,48},{16,52},{20,56},{24,60},{28,64},{32,6... | collective-permute-start | bytes 18440
  611.7 19.2 %collective-permute-start.23 = (bf16[16,192]{1,0:T(8,128)(2,1)S(1)}, bf16[16,192]{1,0:T(8,128)(2,1)S(1)}, u32[]{:S(2)}, u32[]{:S(2)}) collective-permute-start(bf16[16,192]{1,0:T(8,128)(2,1)S(1)} %convert.108), channel_id=1, source_target_pairs={{0,32},{4,36},{8,40},{12,44},{16,48},{20,52},{24,56},{28,60},{32,6... | collective-permute-start | bytes 18440
  613.0 22.8 %collective-permute-start.22 = (bf16[16,192]{1,0:T(8,128)(2,1)S(1)}, bf16[16,192]{1,0:T(8,128)(2,1)S(1)}, u32[]{:S(2)}, u32[]{:S(2)}) collective-permute-start(bf16[16,192]{1,0:T(8,128)(2,1)S(1)} %convert.108), channel_id=1, source_target_pairs={{0,28},{4,32},{8,36},{12,40},{16,44},{20,48},{24,52},{28,56},{32,6... | collective-permute-start | bytes 18440
  614.3 25.3 %collective-permute-start.21 = (bf16[16,192]{1,0:T(8,128)(2,1)S(1)}, bf16[16,192]{1,0:T(8,128)(2,1)S(1)}, u32[]{:S(2)}, u32[]{:S(2)}) collective-permute-start(bf16[16,192]{1,0:T(8,128)(2,1)S(1)} %convert.108), channel_id=1, source_target_pairs={{0,24},{4,28},{8,32},{12,36},{16,40},{20,44},{24,48},{28,52},{32,5... | collective-permute-start | bytes 18440
  626.4 16.3 %collective-permute-start.20 = (bf16[16,192]{1,0:T(8,128)(2,1)S(1)}, bf16[16,192]{1,0:T(8,128)(2,1)S(1)}, u32[]{:S(2)}, u32[]{:S(2)}) collective-permute-start(bf16[16,192]{1,0:T(8,128)(2,1)S(1)} %convert.108), channel_id=1, source_target_pairs={{0,20},{4,24},{8,28},{12,32},{16,36},{20,40},{24,44},{28,48},{32,5... | collective-permute-start | bytes 18440
  627.8 20.6 %collective-permute-start.19 = (bf16[16,192]{1,0:T(8,128)(2,1)S(1)}, bf16[16,192]{1,0:T(8,128)(2,1)S(1)}, u32[]{:S(2)}, u32[]{:S(2)}) collective-permute-start(bf16[16,192]{1,0:T(8,128)(2,1)S(1)} %convert.108), channel_id=1, source_target_pairs={{0,16},{4,20},{8,24},{12,28},{16,32},{20,36},{24,40},{28,44},{32,4... | collective-permute-start | bytes 18440
  630.9 21.9 %collective-permute-start.18 = (bf16[16,192]{1,0:T(8,128)(2,1)S(1)}, bf16[16,192]{1,0:T(8,128)(2,1)S(1)}, u32[]{:S(2)}, u32[]{:S(2)}) collective-permute-start(bf16[16,192]{1,0:T(8,128)(2,1)S(1)} %convert.108), channel_id=1, source_target_pairs={{0,12},{4,16},{8,20},{12,24},{16,28},{20,32},{24,36},{28,40},{32,4... | collective-permute-start | bytes 18440
  635.8 19.2 %collective-permute-start.17 = (bf16[16,192]{1,0:T(8,128)(2,1)S(1)}, bf16[16,192]{1,0:T(8,128)(2,1)S(1)}, u32[]{:S(2)}, u32[]{:S(2)}) collective-permute-start(bf16[16,192]{1,0:T(8,128)(2,1)S(1)} %convert.108), channel_id=1, source_target_pairs={{0,8},{4,12},{8,16},{12,20},{16,24},{20,28},{24,32},{28,36},{32,40... | collective-permute-start | bytes 18440
  639.6 17.4 %collective-permute-start.16 = (bf16[16,192]{1,0:T(8,128)(2,1)S(1)}, bf16[16,192]{1,0:T(8,128)(2,1)S(1)}, u32[]{:S(2)}, u32[]{:S(2)}) collective-permute-start(bf16[16,192]{1,0:T(8,128)(2,1)S(1)} %convert.108), channel_id=1, source_target_pairs={{0,4},{4,8},{8,12},{12,16},{16,20},{20,24},{24,28},{28,32},{32,36}... | collective-permute-start | bytes 18440
  642.7 17.2 %collective-permute-start.47 = (bf16[768,6]{0,1:T(8,128)(2,1)S(1)}, bf16[768,6]{0,1:T(8,128)(2,1)S(1)}, u32[]{:S(2)}, u32[]{:S(2)}) collective-permute-start(bf16[768,6]{0,1:T(8,128)(2,1)S(1)} %slice.2), channel_id=1, source_target_pairs={{0,64},{4,68},{8,72},{12,76},{16,80},{20,84},{24,88},{28,92},{32,9... | collective-permute-start | bytes 27656
  648.4 18.7 %collective-permute-start.46 = (bf16[768,8]{0,1:T(8,128)(2,1)S(1)}, bf16[768,8]{0,1:T(8,128)(2,1)S(1)}, u32[]{:S(2)}, u32[]{:S(2)}) collective-permute-start(bf16[768,8]{0,1:T(8,128)(2,1)S(1)} %convert.107), channel_id=1, source_target_pairs={{0,60},{4,64},{8,68},{12,72},{16,76},{20,80},{24,84},{28,88},{32,9... | collective-permute-start | bytes 36872
  652.8 15.6 %collective-permute-start.45 = (bf16[768,8]{0,1:T(8,128)(2,1)S(1)}, bf16[768,8]{0,1:T(8,128)(2,1)S(1)}, u32[]{:S(2)}, u32[]{:S(2)}) collective-permute-start(bf16[768,8]{0,1:T(8,128)(2,1)S(1)} %convert.107), channel_id=1, source_target_pairs={{0,56},{4,60},{8,64},{12,68},{16,72},{20,76},{24,80},{28,84},{32,8... | collective-permute-start | bytes 36872
  655.1 16.8 %collective-permute-start.44 = (bf16[768,8]{0,1:T(8,128)(2,1)S(1)}, bf16[768,8]{0,1:T(8,128)(2,1)S(1)}, u32[]{:S(2)}, u32[]{:S(2)}) collective-permute-start(bf16[768,8]{0,1:T(8,128)(2,1)S(1)} %convert.107), channel_id=1, source_target_pairs={{0,52},{4,56},{8,60},{12,64},{16,68},{20,72},{24,76},{28,80},{32,8... | collective-permute-start | bytes 36872
  657.0 16.2 %collective-permute-start.43 = (bf16[768,8]{0,1:T(8,128)(2,1)S(1)}, bf16[768,8]{0,1:T(8,128)(2,1)S(1)}, u32[]{:S(2)}, u32[]{:S(2)}) collective-permute-start(bf16[768,8]{0,1:T(8,128)(2,1)S(1)} %convert.107), channel_id=1, source_target_pairs={{0,48},{4,52},{8,56},{12,60},{16,64},{20,68},{24,72},{28,76},{32,8... | collective-permute-start | bytes 36872
  659.8 16.5 %collective-permute-start.42 = (bf16[768,8]{0,1:T(8,128)(2,1)S(1)}, bf16[768,8]{0,1:T(8,128)(2,1)S(1)}, u32[]{:S(2)}, u32[]{:S(2)}) collective-permute-start(bf16[768,8]{0,1:T(8,128)(2,1)S(1)} %convert.107), channel_id=1, source_target_pairs={{0,44},{4,48},{8,52},{12,56},{16,60},{20,64},{24,68},{28,72},{32,7... | collective-permute-start | bytes 36872
  673.2 16.4 %collective-permute-start.38 = (bf16[768,8]{0,1:T(8,128)(2,1)S(1)}, bf16[768,8]{0,1:T(8,128)(2,1)S(1)}, u32[]{:S(2)}, u32[]{:S(2)}) collective-permute-start(bf16[768,8]{0,1:T(8,128)(2,1)S(1)} %convert.107), channel_id=1, source_target_pairs={{0,28},{4,32},{8,36},{12,40},{16,44},{20,48},{24,52},{28,56},{32,6... | collective-permute-start | bytes 36872
  676.3 16.1 %collective-permute-start.37 = (bf16[768,8]{0,1:T(8,128)(2,1)S(1)}, bf16[768,8]{0,1:T(8,128)(2,1)S(1)}, u32[]{:S(2)}, u32[]{:S(2)}) collective-permute-start(bf16[768,8]{0,1:T(8,128)(2,1)S(1)} %convert.107), channel_id=1, source_target_pairs={{0,24},{4,28},{8,32},{12,36},{16,40},{20,44},{24,48},{28,52},{32,5... | collective-permute-start | bytes 36872
  (51 other events, 1035.8 us)
